TPU v7x, 256 devices: a whole 4x4x8 slice. The times are simulated.
256 devices in a mesh: dp: 32 (over x, y, core), mp: 8 (over z).
Axes of the slice: x: 4, y: 4, z: 8, core: 2. Of those that a mesh axis runs over, the one named last changes fastest.
Arguments:
- queries: bfloat16 [4096, 64, 128], P('dp', 'mp'), may hold values from -6 to 6
- key_cache: bfloat16 [4096, 8, 128, 128], P('dp', 'mp'), may hold values from -6 to 6
- value_cache: bfloat16 [4096, 8, 128, 128], P('dp', 'mp'), may hold values from -6 to 6
- key_new: bfloat16 [4096, 8, 128], P('dp', 'mp'), may hold values from -6 to 6
- value_new: bfloat16 [4096, 8, 128], P('dp', 'mp'), may hold values from -6 to 6
- lengths: int32 [4096], P('dp'), may hold values from 1 to 128, as said below
- occupied: int32 [4096], P('dp'), may hold values 0 or 1
- slot_request: int32 [4096], P('dp'), may hold values from 0 to 4095, as said below
- request_adapter: int32 [4096], replicated, may hold values from 0 to 63, as said below
- out_weight: bfloat16 [8192, 4096], P('mp'), may hold values from -0.375 to 0.375
- shrink_weight: bfloat16 [64, 8192, 64], P('dp', 'mp'), may hold values from -0.375 to 0.375
- expand_weight: bfloat16 [64, 64, 4096], P('dp', None, 'mp'), may hold values from -0.75 to 0.75
Outputs:
- mixed: bfloat16 [4096, 4096], P('dp', 'mp')
Inputs may be any that keep to these rules, and one draw needn't show every extreme that they name: `slot_request`: A permutation: each request stands in exactly one slot. `request_adapter`: adapter n is owned by dp index n // 2. Among the slots of one dp index, at most 8 hold requests whose adapters one dp index owns; in every draw some dp index owns the adapters of exactly 8 slots of every dp index. `lengths`: each dp index has a slot of length 128.
All inputs are finite; a program needn't handle non-finite values. No bound on the sum of `occupied` on one device may be relied on, other than what follows from the above.
Results may differ from a plain program's by a relative error of at most 0.011.
Values may be sent and summed in bfloat16 or wider, within the bound.
A program may use at most 64 MiB of HBM per device.

v0:
```python
import math

import jax
import jax.numpy as jnp
from jax import lax
from jax.sharding import PartitionSpec as P


def attend(queries, key_cache, value_cache, key_new, value_new, lengths):
    rows, heads, width = queries.shape
    kv_local = key_cache.shape[1]
    group = heads // kv_local
    inverse = 1.0 / math.sqrt(width)
    grouped = queries.reshape(rows, kv_local, group, width)
    cached = (
        jnp.einsum("bgjd,bgtd->bgjt", grouped, key_cache, preferred_element_type=jnp.float32)
        * inverse
    )
    fresh = (
        jnp.einsum("bgjd,bgd->bgj", grouped, key_new, preferred_element_type=jnp.float32) * inverse
    )
    valid = jnp.arange(key_cache.shape[2])[None, :] < lengths[:, None]
    cached = jnp.where(valid[:, None, None, :], cached, -jnp.inf)
    top = jnp.maximum(jnp.max(cached, axis=-1), fresh)
    cached_exp = jnp.exp(cached - top[..., None])
    fresh_exp = jnp.exp(fresh - top)
    total = jnp.sum(cached_exp, axis=-1) + fresh_exp
    cached_w = (cached_exp / total[..., None]).astype(jnp.bfloat16)
    fresh_w = (fresh_exp / total).astype(jnp.bfloat16)
    summed = jnp.einsum(
        "bgjt,bgtd->bgjd", cached_w, value_cache, preferred_element_type=jnp.float32
    )
    summed = (
        summed
        + fresh_w.astype(jnp.float32)[..., None] * value_new.astype(jnp.float32)[:, :, None, :]
    )
    return summed.reshape(rows, heads * width).astype(jnp.bfloat16)


def body(
    queries,
    key_cache,
    value_cache,
    key_new,
    value_new,
    lengths,
    occupied,
    slot_request,
    request_adapter,
    out_weight,
    shrink_weight,
    expand_weight,
):
    rows = queries.shape[0]
    attended = attend(queries, key_cache, value_cache, key_new, value_new, lengths)
    owners_count = lax.axis_size("dp")
    adapters_here = shrink_weight.shape[0]
    rank_width = shrink_weight.shape[2]
    out_local = expand_weight.shape[2]
    capacity = 2 * rows // owners_count
    matches = (
        slot_request[:, None] == jnp.arange(request_adapter.shape[0], dtype=jnp.int32)[None, :]
    )
    slot_adapter = jnp.sum(jnp.where(matches, request_adapter[None, :], 0), axis=1)
    owner = slot_adapter // adapters_here
    local_ids = slot_adapter % adapters_here
    owner_onehot = (owner[:, None] == jnp.arange(owners_count, dtype=jnp.int32)[None, :]).astype(
        jnp.int32
    )
    earlier = jnp.cumsum(owner_onehot, axis=0) - owner_onehot
    position = jnp.sum(earlier * owner_onehot, axis=1)
    slot_code = owner * capacity + position
    dispatch = jnp.arange(owners_count * capacity, dtype=jnp.int32)[:, None] == slot_code[None, :]
    send_rows = jnp.dot(
        dispatch.astype(jnp.bfloat16), attended, preferred_element_type=jnp.float32
    ).astype(jnp.bfloat16)
    send_rows = send_rows.reshape(owners_count, capacity, attended.shape[1])
    send_ids = jnp.sum(jnp.where(dispatch, (local_ids + 1)[None, :], 0), axis=1).reshape(
        owners_count, capacity
    )
    combine = (
        slot_code[:, None] == jnp.arange(owners_count * capacity, dtype=jnp.int32)[None, :]
    ).astype(jnp.bfloat16)
    partial_value = jnp.dot(attended, out_weight, preferred_element_type=jnp.float32)
    full = lax.psum(partial_value, "mp")
    base = lax.dynamic_slice_in_dim(full, lax.axis_index("mp") * out_local, out_local, 1)
    got_rows = lax.all_to_all(send_rows, "dp", split_axis=0, concat_axis=0, tiled=True)
    got_ids = lax.all_to_all(send_ids, "dp", split_axis=0, concat_axis=0, tiled=True)
    flat = got_rows.reshape(owners_count * capacity, got_rows.shape[2])
    wanted = got_ids.reshape(owners_count * capacity) - 1
    partial_value = jnp.einsum(
        "md,adr->mar", flat, shrink_weight, preferred_element_type=jnp.float32
    )
    which = jnp.arange(adapters_here, dtype=jnp.int32)[None, :] == wanted[:, None]
    partial_value = jnp.where(which[:, :, None], partial_value, 0.0)
    summed = lax.psum(
        partial_value.reshape(owners_count * capacity, adapters_here * rank_width), "mp"
    )
    low = summed.astype(jnp.bfloat16).reshape(owners_count * capacity, adapters_here, rank_width)
    delta = 0.5 * jnp.einsum("mar,are->me", low, expand_weight, preferred_element_type=jnp.float32)
    delta = delta.astype(jnp.bfloat16).reshape(owners_count, capacity, out_local)
    back = lax.all_to_all(delta, "dp", split_axis=0, concat_axis=0, tiled=True)
    correction = jnp.dot(
        combine,
        back.reshape(owners_count * capacity, out_local),
        preferred_element_type=jnp.float32,
    )
    return (occupied.astype(jnp.float32)[:, None] * (base + correction)).astype(jnp.bfloat16)


def solution(mesh):
    placed = (
        P("dp", "mp", None),
        P("dp", "mp", None, None),
        P("dp", "mp", None, None),
        P("dp", "mp", None),
        P("dp", "mp", None),
        P("dp"),
        P("dp"),
        P("dp"),
        P(),
        P("mp", None),
        P("dp", "mp", None),
        P("dp", None, "mp"),
    )
    return jax.shard_map(body, mesh=mesh, in_specs=placed, out_specs=P("dp", "mp"), check_vma=False)
```

profile of v0, /device:TPU:22, one launch (start us, length us, event | category | flops | bytes accessed | tf_op | source)
XLA Modules:
  0.0 117.1 jit_solution(17132844115245272164)
XLA Ops:
  6.5 0.0 copy-start
  6.5 0.0 copy-start.1
  6.5 0.0 copy-start.6
  6.5 0.0 copy-start.3
  6.5 0.0 all-reduce.3.cloned.1.call-start
  6.6 0.8 iota_compare_fusion.6
  7.4 4.6 %fusion.42 = (f32[128,8]{1,0:T(8,128)S(1)}, f32[128,8,128]{2,1,0:T(8,128)S(1)}) fusion(bf16[128,8,128]{2,1,0:T(8,128)(2,1)} %param.12, bf16[128,1,128,128]{3,2,1,0:T(8,128)(2,1)} %param.13, pred[128,128]{1,0:T(8,128)(4,1)S(1)} %iota_compare_fusion.6), kind=kOutput, calls=%fused_computation.60 | convolution fusion | flops 33946624 | bytes 5001216 | tf_op jit(solution)/shard_map/bgjd,bgtd->bgjt/dot_general | solution.py:16
  12.0 0.1 copy.19
  12.1 0.0 copy-done.1
  12.1 0.0 copy-done.6
  12.1 0.3 fusion.36
  12.4 0.1 copy.20
  12.6 0.4 fusion.24
  13.0 0.1 copy.22
  13.1 0.1 copy.23
  13.2 0.0 copy-done.3
  13.3 3.5 %fusion.16 = bf16[128,8,128]{2,1,0:T(8,128)(2,1)S(1)} fusion(bf16[128,1,128,128]{3,2,1,0:T(8,128)(2,1)} %param.14, f32[128,8,128]{2,1,0:T(8,128)S(1)} %get-tuple-element.10, f32[128,128]{1,0:T(8,128)S(1)} %bitcast_convert_fusion, f32[128,8]{1,0:T(8,128)S(1)} %copy.23, f32[128,8]{1,0:T(8,128)S(1)} %copy.22, f32[128,8]{1,0:T(8,128)S(1)} %copy.20), kind=kOutput, calls=%fused_computation.14 | convolution fusion | flops 34340864 | bytes 5058560 | tf_op jit(solution)/shard_map/bgjt,bgtd->bgjd/dot_general | solution.py:30
  16.7 0.0 copy-start.4
  16.7 0.0 copy-start.5
  16.7 6.0 %fusion.26 = f32[128,4096]{1,0:T(8,128)} fusion(bf16[1024,4096]{1,0:T(8,128)(2,1)} %param.21, bf16[16,8,8,128]{3,2,1,0:T(8,128)(2,1)S(1)} %bitcast.75), kind=kOutput, calls=%fused_computation.25 | convolution fusion | flops 1073741824 | bytes 10747904 | tf_op jit(solution)/shard_map/dot_general | solution.py:84
  22.7 0.0 copy-start.2
  22.7 0.0 copy-start.7
  22.7 0.0 all-reduce.3.cloned.1.call-update
  22.7 0.0 copy-done.4
  22.8 0.0 copy-done.5
  22.8 0.4 select_reduce_fusion
  23.2 0.1 fusion.35
  23.3 0.2 reduce_window_sum.11
  23.5 0.2 select_reduce_fusion.2
  23.7 0.1 select_reduce_fusion.1
  23.8 0.7 all_to_all.12
  24.5 7.4 %all-to-all-start = ((s32[32,1,8]{2,1,0:T(1,128)}), s32[32,1,8]{2,1,0:T(1,128)S(1)}, u32[]{:S(2)}, u32[]{:S(2)}) async-start(s32[32,1,8]{2,1,0:T(1,128)} %bitcast.6), calls=%async_computation | async-start | bytes 32768 | tf_op jit(solution)/shard_map/all_to_all | solution.py:88
  31.9 1.1 fusion.4
  33.0 2.5 %all-to-all-done = s32[32,1,8]{2,1,0:T(1,128)S(1)} async-done(((s32[32,1,8]{2,1,0:T(1,128)}), s32[32,1,8]{2,1,0:T(1,128)S(1)}, u32[]{:S(2)}, u32[]{:S(2)}) %all-to-all-start) | async-done | bytes 1056 | tf_op jit(solution)/shard_map/all_to_all | solution.py:88
  35.4 7.6 %all-to-all-start.1 = ((bf16[32,8,1024]{2,1,0:T(8,128)(2,1)}), bf16[32,8,1024]{2,1,0:T(8,128)(2,1)S(1)}, u32[]{:S(2)}, u32[]{:S(2)}) async-start(bf16[32,8,1024]{2,1,0:T(8,128)(2,1)} %fusion.4), calls=%async_computation.1 | async-start | bytes 1048576 | tf_op jit(solution)/shard_map/all_to_all | solution.py:87
  43.1 0.1 sub.34
  43.2 7.9 %all-to-all-done.1 = bf16[32,8,1024]{2,1,0:T(8,128)(2,1)S(1)} async-done(((bf16[32,8,1024]{2,1,0:T(8,128)(2,1)}), bf16[32,8,1024]{2,1,0:T(8,128)(2,1)S(1)}, u32[]{:S(2)}, u32[]{:S(2)}) %all-to-all-start.1) | async-done | bytes 524320 | tf_op jit(solution)/shard_map/all_to_all | solution.py:87
  51.1 0.0 copy-done
  51.1 0.3 fusion.22
  51.5 34.2 %all-reduce.4 = bf16[256,128]{0,1:T(8,128)(2,1)S(1)} all-reduce(f32[256,128]{0,1:T(8,128)S(1)} %bitcast.78), channel_id=1, replica_groups=mesh['dp'=32,'mp'=8] {'mp'}, use_global_device_ids=true, to_apply=%region_7.8 | all-reduce | flops 32768 | bytes 196608 | tf_op jit(solution)/shard_map/psum | solution.py:96
  85.7 0.0 copy-done.2
  85.7 0.9 fusion.19
  86.6 7.1 %all-to-all-start.2 = ((bf16[32,8,512]{2,1,0:T(8,128)(2,1)}), bf16[32,8,512]{2,1,0:T(8,128)(2,1)S(1)}, u32[]{:S(2)}, u32[]{:S(2)}) async-start(bf16[32,8,512]{2,1,0:T(8,128)(2,1)} %fusion.19), calls=%async_computation.2 | async-start | bytes 524288 | tf_op jit(solution)/shard_map/all_to_all | solution.py:102
  93.8 0.0 copy-done.7
  93.8 5.3 %all-to-all-done.2 = bf16[32,8,512]{2,1,0:T(8,128)(2,1)S(1)} async-done(((bf16[32,8,512]{2,1,0:T(8,128)(2,1)}), bf16[32,8,512]{2,1,0:T(8,128)(2,1)S(1)}, u32[]{:S(2)}, u32[]{:S(2)}) %all-to-all-start.2) | async-done | bytes 262176 | tf_op jit(solution)/shard_map/all_to_all | solution.py:102
  99.1 9.4 %all-reduce.3.cloned.1.call-done = f32[128,4096]{1,0:T(8,128)} async-done(((f32[128,4096]{1,0:T(8,128)}), f32[128,4096]{1,0:T(8,128)}) %all-reduce.3.cloned.1.call-update) | async-done | bytes 2097168 | tf_op jit(solution)/shard_map/psum | solution.py:85
  108.5 1.8 %fusion.21 = bf16[128,512]{1,0:T(8,128)(2,1)} fusion(bf16[32,8,512]{2,1,0:T(8,128)(2,1)S(1)} %all-to-all-done.2, f32[128,4096]{1,0:T(8,128)} %all-reduce.3.cloned.1.call-done, s32[]{:T(128)S(6)} %select_n.48, f32[128]{0:T(128)S(1)} %convert_element_type.39, s32[128]{0:T(128)S(1)} %multiply_add_fusion), kind=kOutput, calls=%fused_computation.18 | convolution fusion | flops 33783808 | bytes 656388 | tf_op jit(solution)/shard_map/dot_general | solution.py:103
  (11 shorter events, 0.2 us)
Async XLA Ops:
  6.5 44.6 %copy-start = (bf16[2,1024,64]{1,2,0:T(8,128)(2,1)S(1)}, bf16[2,1024,64]{1,2,0:T(8,128)(2,1)}, u32[]{:S(2)}) copy-start(bf16[2,1024,64]{1,2,0:T(8,128)(2,1)} %param.22) | copy-start | bytes 786436
  6.5 5.5 %copy-start.1 = (bf16[128,8,128]{2,1,0:T(8,128)(2,1)S(1)}, bf16[128,8,128]{2,1,0:T(8,128)(2,1)}, u32[]{:S(2)}) copy-start(bf16[128,8,128]{2,1,0:T(8,128)(2,1)} %param.12) | copy-start | bytes 786436
  6.5 5.5 %copy-start.6 = (bf16[128,1,128]{2,0,1:T(8,128)(2,1)S(1)}, bf16[128,1,128]{2,0,1:T(8,128)(2,1)}, u32[]{:S(2)}) copy-start(bf16[128,1,128]{2,0,1:T(8,128)(2,1)} %param.15) | copy-start | bytes 98308
  6.5 6.7 %copy-start.3 = (bf16[128,1,128]{2,0,1:T(8,128)(2,1)S(1)}, bf16[128,1,128]{2,0,1:T(8,128)(2,1)}, u32[]{:S(2)}) copy-start(bf16[128,1,128]{2,0,1:T(8,128)(2,1)} %param.16) | copy-start | bytes 98308
  6.5 101.9 %all-reduce.3.cloned.1.call-start = ((), (), s32[]{:S(2)}) async-start(), calls=%async_computation.3 | async-start | bytes 4194304 | tf_op jit(solution)/shard_map/psum | solution.py:85
  16.7 6.0 %copy-start.4 = (s32[4096]{0:T(1024)S(1)}, s32[4096]{0:T(1024)}, u32[]{:S(2)}) copy-start(s32[4096]{0:T(1024)} %param.20) | copy-start | bytes 49156
  16.7 6.0 %copy-start.5 = (s32[128]{0:T(128)S(1)}, s32[128]{0:T(128)}, u32[]{:S(2)}) copy-start(s32[128]{0:T(128)} %param.19) | copy-start | bytes 1540
  22.7 63.0 %copy-start.2 = (bf16[2,64,512]{2,1,0:T(8,128)(2,1)S(1)}, bf16[2,64,512]{2,1,0:T(8,128)(2,1)}, u32[]{:S(2)}) copy-start(bf16[2,64,512]{2,1,0:T(8,128)(2,1)} %param.23) | copy-start | bytes 393220
  22.7 71.1 %copy-start.7 = (s32[128]{0:T(128)S(1)}, s32[128]{0:T(128)}, u32[]{:S(2)}) copy-start(s32[128]{0:T(128)} %param.18) | copy-start | bytes 1540
  24.5 11.0 %all-to-all-start = ((s32[32,1,8]{2,1,0:T(1,128)}), s32[32,1,8]{2,1,0:T(1,128)S(1)}, u32[]{:S(2)}, u32[]{:S(2)}) async-start(s32[32,1,8]{2,1,0:T(1,128)} %bitcast.6), calls=%async_computation | async-start | bytes 32768 | tf_op jit(solution)/shard_map/all_to_all | solution.py:88
  35.4 15.7 %all-to-all-start.1 = ((bf16[32,8,1024]{2,1,0:T(8,128)(2,1)}), bf16[32,8,1024]{2,1,0:T(8,128)(2,1)S(1)}, u32[]{:S(2)}, u32[]{:S(2)}) async-start(bf16[32,8,1024]{2,1,0:T(8,128)(2,1)} %fusion.4), calls=%async_computation.1 | async-start | bytes 1048576 | tf_op jit(solution)/shard_map/all_to_all | solution.py:87
  86.6 12.4 %all-to-all-start.2 = ((bf16[32,8,512]{2,1,0:T(8,128)(2,1)}), bf16[32,8,512]{2,1,0:T(8,128)(2,1)S(1)}, u32[]{:S(2)}, u32[]{:S(2)}) async-start(bf16[32,8,512]{2,1,0:T(8,128)(2,1)} %fusion.19), calls=%async_computation.2 | async-start | bytes 524288 | tf_op jit(solution)/shard_map/all_to_all | solution.py:102
Sparse Core Ops, SparseCore 0:
  22.9 85.5 all-reduce.2
where the time goes:
time: 118 us; the launch traced here: 117 us
  blocking collectives  34.2 us (29%)
  waiting for transfers between devices  25.1 us (21%)
  starting transfers between devices  22.2 us (19%)
  matrix products  18.5 us (16%)
  between operations  13.6 us (12%)
  other arithmetic  2.26 us (2%)
  local copies, waits for them, and re-layouts  1.31 us (1%)
    psum x1, blocking collectives, body(): lax.psum(partial_value.reshape(owners_count * capacity, adapters_here * r...  34.2 us
    psum x1, waiting for transfers between devices, body(): full = lax.psum(partial_value, 'mp')  9.39 us
    all_to_all x1, waiting for transfers between devices, body(): lax.all_to_all(send_rows, 'dp', split_axis=0, concat_axis=0, tiled=True)  7.91 us
    all_to_all x1, starting transfers between devices, body(): lax.all_to_all(send_rows, 'dp', split_axis=0, concat_axis=0, tiled=True)  7.63 us
    all_to_all x1, starting transfers between devices, body(): lax.all_to_all(send_ids, 'dp', split_axis=0, concat_axis=0, tiled=True)  7.41 us
    all_to_all x1, starting transfers between devices, body(): back = lax.all_to_all(delta, 'dp', split_axis=0, concat_axis=0, tiled=True)  7.14 us
    dot_general x1, matrix products, body(): jnp.dot(attended, out_weight, preferred_element_type=jnp.float32)  5.97 us
    all_to_all x1, waiting for transfers between devices, body(): back = lax.all_to_all(delta, 'dp', split_axis=0, concat_axis=0, tiled=True)  5.27 us
  transfers between devices with their start and end apart: 4, of which 4 were waited for; matrix products, arithmetic and copies ran while one was open for 3% of the time, Pallas kernels for 0%

commit v1 on v0

v1 whole, which is shorter than its diff:
```python
import functools
import math

import jax
import jax.numpy as jnp
from jax import lax
from jax.experimental import pallas as pl
from jax.experimental.pallas import tpu as pltpu
from jax.sharding import PartitionSpec as P

MESH = pl.DeviceIdType.MESH
BF = jnp.bfloat16
F32 = jnp.float32
CHUNK = 16


def nt_dot(a, b):
    return lax.dot_general(a, b, (((1,), (1,)), ((), ())), preferred_element_type=F32)


def nn_dot(a, b):
    return jnp.dot(a, b, preferred_element_type=F32)


def chain_messages(half):
    messages = [(half, 0)]
    for left in range(half - 1, 0, -1):
        messages += [(left, 1), (left, 0)]
    return messages


def kernel(
    n,
    mp,
    cap,
    lens_hbm,
    occ_hbm,
    sreq_hbm,
    radp_hbm,
    q_hbm,
    k_hbm,
    v_hbm,
    kn_hbm,
    vn_hbm,
    w_hbm,
    shr_hbm,
    exp_hbm,
    out_ref,
    lens,
    occ,
    sreq,
    radp,
    qbuf,
    kbuf,
    vbuf,
    knb,
    vnb,
    knf,
    vnf,
    wbuf,
    shr,
    expw,
    obuf,
    att,
    disp,
    comb,
    ids_out,
    ids_in,
    rows_out,
    rows_in,
    part,
    msg_out,
    msg_in,
    base,
    rs_out,
    rs_in,
    ag_out,
    ag_in,
    back_out,
    back_in,
    small_sem,
    k_sem,
    v_sem,
    w_sem,
    ids_sems,
    rows_sems,
    rs_sems,
    ag_sems,
    back_sems,
    msg_send,
    msg_recv,
):
    d = lax.axis_index("dp")
    m = lax.axis_index("mp")
    slots = lens.shape[1]
    heads = qbuf.shape[0] // slots
    width = qbuf.shape[1]
    outw = expw.shape[1]
    codes = n * cap
    group = codes // mp
    half_group = group // 2
    half = mp // 2
    inverse = 1.0 / math.sqrt(width)
    chunks = slots // CHUNK
    side = slots // 2

    smalls = [
        pltpu.make_async_copy(src, dst, small_sem.at[i])
        for i, (src, dst) in enumerate(
            [
                (lens_hbm, lens),
                (q_hbm, qbuf),
                (kn_hbm, knb),
                (vn_hbm, vnb),
                (sreq_hbm, sreq),
                (radp_hbm, radp),
                (occ_hbm, occ),
                (shr_hbm, shr),
                (exp_hbm, expw),
            ]
        )
    ]

    def k_copy(c):
        rows = pl.ds(c * CHUNK, CHUNK)
        return pltpu.make_async_copy(k_hbm.at[rows], kbuf.at[rows], k_sem.at[c])

    def v_copy(c):
        rows = pl.ds(c * CHUNK, CHUNK)
        return pltpu.make_async_copy(v_hbm.at[rows], vbuf.at[rows], v_sem.at[c])

    offsets = [half]
    for r in range(half - 1, 0, -1):
        offsets += [r, -r]
    offsets += [0]

    def w_copy(i):
        block = lax.rem(m + offsets[i] + mp, mp)
        cols = pl.ds(pl.multiple_of(block * outw, outw), outw)
        return pltpu.make_async_copy(w_hbm.at[:, cols], wbuf.at[i], w_sem.at[i])

    for copy in smalls[:4]:
        copy.start()
    k_copy(0).start()
    v_copy(0).start()
    for copy in smalls[4:]:
        copy.start()
    for c in range(1, chunks):
        k_copy(c).start()
        v_copy(c).start()
    for i in range(mp):
        w_copy(i).start()

    barrier = pltpu.get_barrier_semaphore()

    def greet_dp(i, carry):
        pl.semaphore_signal(
            barrier, inc=1, device_id=(lax.rem(d + i, n), m), device_id_type=MESH
        )
        return carry

    def greet_mp(i, carry):
        pl.semaphore_signal(
            barrier, inc=1, device_id=(d, lax.rem(m + i, mp)), device_id_type=MESH
        )
        return carry

    lax.fori_loop(1, n, greet_dp, 0)
    lax.fori_loop(1, mp, greet_mp, 0)

    for copy in smalls:
        copy.wait()

    knf[...] = knb[...].astype(F32)
    vnf[...] = vnb[...].astype(F32)
    request = sreq[...]
    high = request // 128
    low_part = request - high * 128
    lane_rows = lax.broadcasted_iota(jnp.int32, (128, slots), 0)
    hot_low = (lane_rows == low_part).astype(F32).astype(BF)
    table = nn_dot(radp[...].astype(F32).astype(BF), hot_low)
    high_rows = lax.broadcasted_iota(jnp.int32, table.shape, 0)
    adapter = jnp.sum(
        jnp.where(high_rows == high, table, 0.0), axis=0, keepdims=True
    ).astype(jnp.int32)
    owner = adapter // 2
    local_id = adapter - owner * 2
    owner_rows = lax.broadcasted_iota(jnp.int32, (n, slots), 0)
    hot_owner = (owner_rows == owner).astype(F32)
    before = (
        lax.broadcasted_iota(jnp.int32, (slots, slots), 0)
        < lax.broadcasted_iota(jnp.int32, (slots, slots), 1)
    ).astype(F32)
    earlier = nn_dot(hot_owner.astype(BF), before.astype(BF))
    position = jnp.sum(hot_owner * earlier, axis=0, keepdims=True).astype(jnp.int32)
    code = owner * cap + position
    code_rows = lax.broadcasted_iota(jnp.int32, (codes, slots), 0)
    hot_code = (code_rows == code).astype(F32)
    disp[...] = hot_code.astype(BF)
    ids = nn_dot(
        (hot_code * local_id.astype(F32)).astype(BF), jnp.ones((slots, 128), BF)
    )
    ids_out[...] = ids.reshape(n, cap, 128).astype(BF)
    same = lax.broadcasted_iota(
        jnp.int32, (slots, slots), 0
    ) == lax.broadcasted_iota(jnp.int32, (slots, slots), 1)
    code_column = jnp.sum(
        jnp.where(same, code.astype(F32), 0.0), axis=1, keepdims=True
    ).astype(jnp.int32)
    comb[...] = (
        (lax.broadcasted_iota(jnp.int32, (slots, codes), 1) == code_column)
        .astype(F32)
        .astype(BF)
    )
    live = jnp.sum(
        jnp.where(same, occ[...].astype(F32), 0.0), axis=1, keepdims=True
    )

    lanes = lax.broadcasted_iota(jnp.int32, (heads, width), 1)

    def attend(c, carry):
        k_copy(c).wait()
        v_copy(c).wait()
        scores, fresh, new_values = [], [], []
        for p in range(CHUNK // 2):
            slot = c * CHUNK + 2 * p
            queries = qbuf[pl.ds(pl.multiple_of(slot * heads, 16), 2 * heads), :]
            keys = kbuf[pl.ds(slot, 2)].reshape(2 * 128, width)
            both = nt_dot(queries, keys) * inverse
            wide = queries.astype(F32)
            for b in range(2):
                tile = both[b * heads : (b + 1) * heads, b * 128 : (b + 1) * 128]
                scores.append(jnp.where(lanes < lens[0, slot + b], tile, -jnp.inf))
                new_key = knf[pl.ds(slot + b, 1), :]
                fresh.append(
                    jnp.sum(
                        wide[b * heads : (b + 1) * heads] * new_key,
                        axis=1,
                        keepdims=True,
                    )
                )
        scores = jnp.concatenate(scores, axis=0)
        fresh = jnp.concatenate(fresh, axis=0) * inverse
        top = jnp.maximum(jnp.max(scores, axis=1, keepdims=True), fresh)
        scores_exp = jnp.exp(scores - top)
        fresh_exp = jnp.exp(fresh - top)
        total = jnp.sum(scores_exp, axis=1, keepdims=True) + fresh_exp
        scale = 1.0 / total
        weights = scores_exp * scale
        fresh_w = (fresh_exp * scale).astype(BF).astype(F32)
        blank = jnp.zeros((heads, 128), F32)
        for p in range(CHUNK // 2):
            slot = c * CHUNK + 2 * p
            r = 2 * p * heads
            pair = jnp.concatenate(
                [
                    jnp.concatenate([weights[r : r + heads], blank], axis=1),
                    jnp.concatenate([blank, weights[r + heads : r + 2 * heads]], axis=1),
                ],
                axis=0,
            ).astype(BF)
            values = vbuf[pl.ds(slot, 2)].reshape(2 * 128, width)
            summed = nn_dot(pair, values)
            for b in range(2):
                new_value = vnf[pl.ds(slot + b, 1), :]
                q = r + b * heads
                obuf[pl.ds(pl.multiple_of((slot + b) * heads, heads), heads), :] = (
                    summed[b * heads : (b + 1) * heads]
                    + fresh_w[q : q + heads] * new_value
                )
        return carry

    first = chunks // 2
    lax.fori_loop(0, first, attend, 0)

    pl.semaphore_wait(barrier, n - 1 + mp - 1)

    def to_owner(out, landing, sems):
        def copy(i):
            peer = lax.rem(d + i, n)
            return pltpu.make_async_remote_copy(
                src_ref=out.at[peer],
                dst_ref=landing.at[d],
                send_sem=sems.at[0, i],
                recv_sem=sems.at[1, i],
                device_id=(peer, m),
                device_id_type=MESH,
            )

        return copy

    def over_mp(out, landing, sems, same_for_all):
        def copy(i):
            peer = lax.rem(m + i, mp)
            return pltpu.make_async_remote_copy(
                src_ref=out if same_for_all else out.at[peer],
                dst_ref=landing.at[m],
                send_sem=sems.at[0, i],
                recv_sem=sems.at[1, i],
                device_id=(d, peer),
                device_id_type=MESH,
            )

        return copy

    def start_all(copy, count):
        def go(i, carry):
            copy(i).start()
            return carry

        lax.fori_loop(1, count, go, 0)

    def recv_all(copy, count):
        def go(i, carry):
            copy(i).wait_recv()
            return carry

        lax.fori_loop(1, count, go, 0)

    def sent_all(copy, count):
        def go(i, carry):
            copy(i).wait_send()
            return carry

        lax.fori_loop(1, count, go, 0)

    ids_copy = to_owner(ids_out, ids_in, ids_sems)
    rows_copy = to_owner(rows_out, rows_in, rows_sems)
    back_copy = to_owner(back_out, back_in, back_sems)
    rs_copy = over_mp(rs_out, rs_in, rs_sems, False)
    ag_copy = over_mp(ag_out, ag_in, ag_sems, True)

    start_all(ids_copy, n)
    lax.fori_loop(first, chunks, attend, 0)
    ids_in[d] = ids_out[d]

    for j in range(heads):
        cols = pl.ds(j * width, width)
        head = obuf[pl.ds(j, slots, stride=heads), :].astype(BF)
        att[:, cols] = head
        sent = nn_dot(disp[...], head)
        rows_out[:, :, cols] = sent.reshape(n, cap, width).astype(BF)
    start_all(rows_copy, n)

    def block_product(i):
        w_copy(i).wait()
        part[i] = nn_dot(att[...], wbuf[i])

    messages = chain_messages(half)
    where = {message: i for i, message in enumerate(messages)}

    def slot_of(direction, left):
        return offsets.index(left if direction == 0 or left in (0, half) else -left)

    def lane_rows_of(direction, lane):
        upper = lane if direction == 0 else 1 - lane
        return pl.ds(upper * side, side)

    def msg_copy(direction, i):
        peer = lax.rem(m + (1 if direction == 0 else mp - 1), mp)
        return pltpu.make_async_remote_copy(
            src_ref=msg_out.at[direction, i],
            dst_ref=msg_in.at[direction, i],
            send_sem=msg_send.at[direction, i],
            recv_sem=msg_recv.at[direction, i],
            device_id=(d, peer),
            device_id_type=MESH,
        )

    def send_message(i):
        left, lane = messages[i]
        for direction in range(2):
            rows = lane_rows_of(direction, lane)
            value = part[slot_of(direction, left), rows, :]
            came = where.get((left + 1, lane))
            if came is not None:
                msg_copy(direction, came).wait_recv()
                value = value + msg_in[direction, came].astype(F32)
            msg_out[direction, i] = value.astype(BF)
            msg_copy(direction, i).start()

    def finish_base():
        for lane in range(2):
            last = where[(1, lane)] if (1, lane) in where else None
            if last is None:
                continue
            for direction in range(2):
                rows = lane_rows_of(direction, lane)
                msg_copy(direction, last).wait_recv()
                base[rows, :] += msg_in[direction, last].astype(F32)

    def share_rows():
        recv_all(ids_copy, n)
        rows_in[d] = rows_out[d]
        recv_all(rows_copy, n)
        got = rows_in[...].astype(F32).reshape(codes, rows_in.shape[2]).astype(BF)
        partial_low = nt_dot(got, shr[...])
        which = ids_in[...].astype(F32).reshape(codes, 128)
        row = lax.broadcasted_iota(jnp.int32, (codes, 128), 0)
        second = ((row // half_group) % 2).astype(F32)
        placed = jnp.where(which == second, partial_low, pltpu.roll(partial_low, 64, 1))
        lane = lax.broadcasted_iota(jnp.int32, (half_group, 128), 1)
        for g in range(mp):
            r = g * group
            rs_out[g] = jnp.where(
                lane < 64,
                placed[r : r + half_group],
                placed[r + half_group : r + group],
            )
        start_all(rs_copy, mp)
        rs_in[m] = rs_out[m]

    def sum_low():
        recv_all(rs_copy, mp)
        ag_out[...] = jnp.sum(rs_in[...], axis=0).astype(BF)
        start_all(ag_copy, mp)
        ag_in[m] = ag_out[...]

    def expand_low():
        recv_all(ag_copy, mp)
        low = ag_in[...].astype(F32)
        twice = jnp.concatenate(
            [low[g] for g in range(mp) for _ in range(2)], axis=0
        )
        which = ids_in[...].astype(F32).reshape(codes, 128)
        row = lax.broadcasted_iota(jnp.int32, (codes, 128), 0)
        second = ((row // half_group) % 2).astype(F32)
        lane_half = (
            lax.broadcasted_iota(jnp.int32, (codes, 128), 1) // 64
        ).astype(F32)
        moved = jnp.where(which == second, twice, pltpu.roll(twice, 64, 1))
        kept = jnp.where(which == lane_half, moved, 0.0).astype(BF)
        delta = 0.5 * nn_dot(kept, expw[...])
        back_out[...] = delta.reshape(n, cap, outw).astype(BF)
        start_all(back_copy, n)
        back_in[d] = back_out[d]

    count = len(messages)
    block_product(0)
    send_message(0)
    block_product(1)
    block_product(2)
    send_message(1)
    block_product(3)
    block_product(4)
    send_message(2)
    block_product(5)
    block_product(6)
    send_message(3)
    w_copy(mp - 1).wait()
    base[...] = nn_dot(att[...], wbuf[mp - 1])
    send_message(4)
    share_rows()
    send_message(5)
    sum_low()
    send_message(6)
    expand_low()
    finish_base()

    recv_all(back_copy, n)
    returned = back_in[...].astype(F32).reshape(codes, outw).astype(BF)
    correction = nn_dot(comb[...], returned)
    out_ref[...] = (live * (base[...] + correction)).astype(BF)

    for copy, total_count in (
        (ids_copy, n),
        (rows_copy, n),
        (back_copy, n),
        (rs_copy, mp),
        (ag_copy, mp),
    ):
        sent_all(copy, total_count)
    for i in range(count):
        for direction in range(2):
            msg_copy(direction, i).wait_send()


def solution(mesh):
    n = mesh.shape["dp"]
    mp = mesh.shape["mp"]

    def body(
        queries,
        key_cache,
        value_cache,
        key_new,
        value_new,
        lengths,
        occupied,
        slot_request,
        request_adapter,
        out_weight,
        shrink_weight,
        expand_weight,
    ):
        slots, heads, width = queries.shape
        cached = key_cache.shape[2]
        features = heads * width
        outw = expand_weight.shape[2]
        cap = 2 * slots // n
        codes = n * cap
        ranks = shrink_weight.shape[0] * shrink_weight.shape[2]
        requests = request_adapter.shape[0]
        chunks = slots // CHUNK
        messages = 2 * (mp // 2) - 1
        packed = codes // mp // 2
        any_spec = pl.BlockSpec(memory_space=pl.ANY)
        dma = pltpu.SemaphoreType.DMA
        return pl.pallas_call(
            functools.partial(kernel, n, mp, cap),
            out_shape=jax.ShapeDtypeStruct((slots, outw), BF),
            in_specs=[any_spec] * 12,
            out_specs=pl.BlockSpec(memory_space=pltpu.VMEM),
            scratch_shapes=[
                pltpu.SMEM((1, slots), jnp.int32),
                pltpu.VMEM((1, slots), jnp.int32),
                pltpu.VMEM((1, slots), jnp.int32),
                pltpu.VMEM((requests // 128, 128), jnp.int32),
                pltpu.VMEM((slots * heads, width), BF),
                pltpu.VMEM((slots, cached, width), BF),
                pltpu.VMEM((slots, cached, width), BF),
                pltpu.VMEM((slots, width), BF),
                pltpu.VMEM((slots, width), BF),
                pltpu.VMEM((slots, width), F32),
                pltpu.VMEM((slots, width), F32),
                pltpu.VMEM((mp, features, outw), BF),
                pltpu.VMEM((ranks, features), BF),
                pltpu.VMEM((ranks, outw), BF),
                pltpu.VMEM((slots * heads, width), F32),
                pltpu.VMEM((slots, features), BF),
                pltpu.VMEM((codes, slots), BF),
                pltpu.VMEM((slots, codes), BF),
                pltpu.VMEM((n, cap, 128), BF),
                pltpu.VMEM((n, cap, 128), BF),
                pltpu.VMEM((n, cap, features), BF),
                pltpu.VMEM((n, cap, features), BF),
                pltpu.VMEM((mp, slots, outw), F32),
                pltpu.VMEM((2, messages, slots // 2, outw), BF),
                pltpu.VMEM((2, messages, slots // 2, outw), BF),
                pltpu.VMEM((slots, outw), F32),
                pltpu.VMEM((mp, packed, 128), F32),
                pltpu.VMEM((mp, packed, 128), F32),
                pltpu.VMEM((packed, 128), BF),
                pltpu.VMEM((mp, packed, 128), BF),
                pltpu.VMEM((n, cap, outw), BF),
                pltpu.VMEM((n, cap, outw), BF),
                dma((9,)),
                dma((chunks,)),
                dma((chunks,)),
                dma((mp,)),
                dma((2, n)),
                dma((2, n)),
                dma((2, mp)),
                dma((2, mp)),
                dma((2, n)),
                dma((2, messages)),
                dma((2, messages)),
            ],
            compiler_params=pltpu.CompilerParams(
                collective_id=0,
                has_side_effects=True,
                vmem_limit_bytes=48 << 20,
            ),
        )(
            lengths.reshape(1, slots),
            occupied.reshape(1, slots),
            slot_request.reshape(1, slots),
            request_adapter.reshape(requests // 128, 128),
            queries.reshape(slots * heads, width),
            key_cache.reshape(slots, cached, width),
            value_cache.reshape(slots, cached, width),
            key_new.reshape(slots, width),
            value_new.reshape(slots, width),
            out_weight,
            shrink_weight.transpose(0, 2, 1).reshape(ranks, features),
            expand_weight.reshape(ranks, outw),
        )

    placed = (
        P("dp", "mp", None),
        P("dp", "mp", None, None),
        P("dp", "mp", None, None),
        P("dp", "mp", None),
        P("dp", "mp", None),
        P("dp"),
        P("dp"),
        P("dp"),
        P(),
        P("mp", None),
        P("dp", "mp", None),
        P("dp", None, "mp"),
    )
    return jax.shard_map(
        body, mesh=mesh, in_specs=placed, out_specs=P("dp", "mp"), check_vma=False
    )
```

time: 118 us -> 54.6 us (0.46)
  the two profiles are of different devices: /device:TPU:22 before, /device:TPU:1 now
where the time goes in v1:
time: 54.6 us; the launch traced here: 54.1 us
  Pallas kernels  44.3 us (81%)
  local copies, waits for them, and re-layouts  9.84 us (18%)
    pallas_call x1, Pallas kernels, body(): pl.pallas_call(functools.partial(kernel, n, mp, cap), out_shape=jax.Shape...  44.3 us
    unnamed x21, local copies, waits for them, and re-layouts  9.84 us

profile of v1, /device:TPU:1, one launch (start us, length us, event | category | flops | bytes accessed | tf_op | source)
XLA Modules:
  0.0 54.1 jit_solution(10679873092221539797)
XLA Ops:
  0.0 0.0 copy-start
  0.0 2.2 %copy-done = bf16[128,1,128,128]{3,2,1,0:T(8,128)(2,1)S(1)} copy-done((bf16[128,1,128,128]{3,2,1,0:T(8,128)(2,1)S(1)}, bf16[128,1,128,128]{3,2,1,0:T(8,128)(2,1)}, u32[]{:S(2)}) %copy-start) | copy-done | bytes 4194328
  2.2 0.0 copy-start.1
  2.2 0.9 %copy-done.1 = bf16[128,8,128]{2,1,0:T(8,128)(2,1)S(1)} copy-done((bf16[128,8,128]{2,1,0:T(8,128)(2,1)S(1)}, bf16[128,8,128]{2,1,0:T(8,128)(2,1)}, u32[]{:S(2)}) %copy-start.1) | copy-done | bytes 262168
  3.1 0.0 copy-start.2
  3.1 0.9 %copy-done.2 = bf16[2,1024,64]{1,2,0:T(8,128)(2,1)S(1)} copy-done((bf16[2,1024,64]{1,2,0:T(8,128)(2,1)S(1)}, bf16[2,1024,64]{1,2,0:T(8,128)(2,1)}, u32[]{:S(2)}) %copy-start.2) | copy-done | bytes 262168
  4.1 0.0 copy-start.3
  4.1 0.9 %copy-done.3 = bf16[2,64,512]{2,1,0:T(8,128)(2,1)S(1)} copy-done((bf16[2,64,512]{2,1,0:T(8,128)(2,1)S(1)}, bf16[2,64,512]{2,1,0:T(8,128)(2,1)}, u32[]{:S(2)}) %copy-start.3) | copy-done | bytes 131096
  5.0 0.0 copy-start.4
  5.0 0.8 %copy-done.4 = bf16[128,1,128]{2,0,1:T(8,128)(2,1)S(1)} copy-done((bf16[128,1,128]{2,0,1:T(8,128)(2,1)S(1)}, bf16[128,1,128]{2,0,1:T(8,128)(2,1)}, u32[]{:S(2)}) %copy-start.4) | copy-done | bytes 32792
  5.8 0.0 copy-start.5
  5.8 0.8 %copy-done.5 = bf16[128,1,128]{2,0,1:T(8,128)(2,1)S(1)} copy-done((bf16[128,1,128]{2,0,1:T(8,128)(2,1)S(1)}, bf16[128,1,128]{2,0,1:T(8,128)(2,1)}, u32[]{:S(2)}) %copy-start.5) | copy-done | bytes 32792
  6.5 0.0 copy-start.6
  6.5 0.7 %copy-done.6 = s32[4096]{0:T(1024)S(1)} copy-done((s32[4096]{0:T(1024)S(1)}, s32[4096]{0:T(1024)}, u32[]{:S(2)}) %copy-start.6) | copy-done | bytes 16408
  7.2 0.0 copy-start.7
  7.2 0.7 %copy-done.7 = s32[128]{0:T(128)S(1)} copy-done((s32[128]{0:T(128)S(1)}, s32[128]{0:T(128)}, u32[]{:S(2)}) %copy-start.7) | copy-done | bytes 536
  7.9 0.0 copy-start.8
  7.9 0.7 %copy-done.8 = s32[128]{0:T(128)S(1)} copy-done((s32[128]{0:T(128)S(1)}, s32[128]{0:T(128)}, u32[]{:S(2)}) %copy-start.8) | copy-done | bytes 536
  8.5 0.0 copy-start.9
  8.5 0.7 %copy-done.9 = s32[128]{0:T(128)S(1)} copy-done((s32[128]{0:T(128)S(1)}, s32[128]{0:T(128)}, u32[]{:S(2)}) %copy-start.9) | copy-done | bytes 536
  9.2 44.3 %shard_map.118 = bf16[128,512]{1,0:T(8,128)(2,1)S(1)} custom-call(s32[1,128]{1,0:T(1,128)S(1)} %bitcast.20, s32[1,128]{1,0:T(1,128)S(1)} %bitcast.21, s32[1,128]{1,0:T(1,128)S(1)} %bitcast.22, s32[32,128]{1,0:T(8,128)S(1)} %bitcast.19, bf16[1024,128]{1,0:T(8,128)(2,1)S(1)} %bitcast.14, bf16[128,128,128]{2,1,0:T(8,128)(2,1)S(1)} %bitcast.13, ...), custom_call_target="tpu_custom_call" | custom-call | tf_op jit(solution)/shard_map/pallas_call | solution.py:509
  53.5 0.7 %copy.14 = bf16[128,512]{1,0:T(8,128)(2,1)} copy(bf16[128,512]{1,0:T(8,128)(2,1)S(1)} %shard_map.118) | data formatting | bytes 262144
Async XLA Ops:
  0.0 2.2 %copy-start = (bf16[128,1,128,128]{3,2,1,0:T(8,128)(2,1)S(1)}, bf16[128,1,128,128]{3,2,1,0:T(8,128)(2,1)}, u32[]{:S(2)}) copy-start(bf16[128,1,128,128]{3,2,1,0:T(8,128)(2,1)} %param.13) | copy-start | bytes 12582916
  2.2 0.9 %copy-start.1 = (bf16[128,8,128]{2,1,0:T(8,128)(2,1)S(1)}, bf16[128,8,128]{2,1,0:T(8,128)(2,1)}, u32[]{:S(2)}) copy-start(bf16[128,8,128]{2,1,0:T(8,128)(2,1)} %param.12) | copy-start | bytes 786436
  3.1 0.9 %copy-start.2 = (bf16[2,1024,64]{1,2,0:T(8,128)(2,1)S(1)}, bf16[2,1024,64]{1,2,0:T(8,128)(2,1)}, u32[]{:S(2)}) copy-start(bf16[2,1024,64]{1,2,0:T(8,128)(2,1)} %param.22) | copy-start | bytes 786436
  4.1 0.9 %copy-start.3 = (bf16[2,64,512]{2,1,0:T(8,128)(2,1)S(1)}, bf16[2,64,512]{2,1,0:T(8,128)(2,1)}, u32[]{:S(2)}) copy-start(bf16[2,64,512]{2,1,0:T(8,128)(2,1)} %param.23) | copy-start | bytes 393220
  5.0 0.8 %copy-start.4 = (bf16[128,1,128]{2,0,1:T(8,128)(2,1)S(1)}, bf16[128,1,128]{2,0,1:T(8,128)(2,1)}, u32[]{:S(2)}) copy-start(bf16[128,1,128]{2,0,1:T(8,128)(2,1)} %param.15) | copy-start | bytes 98308
  5.8 0.8 %copy-start.5 = (bf16[128,1,128]{2,0,1:T(8,128)(2,1)S(1)}, bf16[128,1,128]{2,0,1:T(8,128)(2,1)}, u32[]{:S(2)}) copy-start(bf16[128,1,128]{2,0,1:T(8,128)(2,1)} %param.16) | copy-start | bytes 98308
  6.5 0.7 %copy-start.6 = (s32[4096]{0:T(1024)S(1)}, s32[4096]{0:T(1024)}, u32[]{:S(2)}) copy-start(s32[4096]{0:T(1024)} %param.20) | copy-start | bytes 49156
  7.2 0.7 %copy-start.7 = (s32[128]{0:T(128)S(1)}, s32[128]{0:T(128)}, u32[]{:S(2)}) copy-start(s32[128]{0:T(128)} %param.17) | copy-start | bytes 1540
  7.9 0.7 %copy-start.8 = (s32[128]{0:T(128)S(1)}, s32[128]{0:T(128)}, u32[]{:S(2)}) copy-start(s32[128]{0:T(128)} %param.18) | copy-start | bytes 1540
  8.5 0.7 %copy-start.9 = (s32[128]{0:T(128)S(1)}, s32[128]{0:T(128)}, u32[]{:S(2)}) copy-start(s32[128]{0:T(128)} %param.19) | copy-start | bytes 1540

commit v2 on v1

--- a/solution.py
+++ b/solution.py
@@ -11,7 +11,6 @@
 MESH = pl.DeviceIdType.MESH
 BF = jnp.bfloat16
 F32 = jnp.float32
-CHUNK = 16
 
 
 def nt_dot(a, b):
@@ -55,8 +54,7 @@
     vbuf,
     knb,
     vnb,
-    knf,
-    vnf,
+    lens_wide,
     wbuf,
     shr,
     expw,
@@ -64,8 +62,6 @@
     att,
     disp,
     comb,
-    ids_out,
-    ids_in,
     rows_out,
     rows_in,
     part,
@@ -82,7 +78,6 @@
     k_sem,
     v_sem,
     w_sem,
-    ids_sems,
     rows_sems,
     rs_sems,
     ag_sems,
@@ -96,12 +91,16 @@
     heads = qbuf.shape[0] // slots
     width = qbuf.shape[1]
     outw = expw.shape[1]
+    features = heads * width
     codes = n * cap
     group = codes // mp
     half_group = group // 2
     half = mp // 2
     inverse = 1.0 / math.sqrt(width)
-    chunks = slots // CHUNK
+    chunk = slots // 2
+    chunks = slots // chunk
+    fetch = slots // 8
+    fetches = slots // fetch
     side = slots // 2
 
     smalls = [
@@ -122,11 +121,11 @@
     ]
 
     def k_copy(c):
-        rows = pl.ds(c * CHUNK, CHUNK)
+        rows = pl.ds(c * fetch, fetch)
         return pltpu.make_async_copy(k_hbm.at[rows], kbuf.at[rows], k_sem.at[c])
 
     def v_copy(c):
-        rows = pl.ds(c * CHUNK, CHUNK)
+        rows = pl.ds(c * fetch, fetch)
         return pltpu.make_async_copy(v_hbm.at[rows], vbuf.at[rows], v_sem.at[c])
 
     offsets = [half]
@@ -135,7 +134,7 @@
     offsets += [0]
 
     def w_copy(i):
-        block = lax.rem(m + offsets[i] + mp, mp)
+        block = (m + offsets[i] + mp) % mp
         cols = pl.ds(pl.multiple_of(block * outw, outw), outw)
         return pltpu.make_async_copy(w_hbm.at[:, cols], wbuf.at[i], w_sem.at[i])
 
@@ -145,23 +144,21 @@
     v_copy(0).start()
     for copy in smalls[4:]:
         copy.start()
-    for c in range(1, chunks):
+    for c in range(1, fetches):
         k_copy(c).start()
         v_copy(c).start()
-    for i in range(mp):
-        w_copy(i).start()
 
     barrier = pltpu.get_barrier_semaphore()
 
     def greet_dp(i, carry):
         pl.semaphore_signal(
-            barrier, inc=1, device_id=(lax.rem(d + i, n), m), device_id_type=MESH
+            barrier, inc=1, device_id=((d + i) % n, m), device_id_type=MESH
         )
         return carry
 
     def greet_mp(i, carry):
         pl.semaphore_signal(
-            barrier, inc=1, device_id=(d, lax.rem(m + i, mp)), device_id_type=MESH
+            barrier, inc=1, device_id=(d, (m + i) % mp), device_id_type=MESH
         )
         return carry
 
@@ -171,8 +168,6 @@
     for copy in smalls:
         copy.wait()
 
-    knf[...] = knb[...].astype(F32)
-    vnf[...] = vnb[...].astype(F32)
     request = sreq[...]
     high = request // 128
     low_part = request - high * 128
@@ -200,7 +195,7 @@
     ids = nn_dot(
         (hot_code * local_id.astype(F32)).astype(BF), jnp.ones((slots, 128), BF)
     )
-    ids_out[...] = ids.reshape(n, cap, 128).astype(BF)
+    rows_out[:, :, features:] = ids.reshape(n, cap, 128).astype(BF)
     same = lax.broadcasted_iota(
         jnp.int32, (slots, slots), 0
     ) == lax.broadcasted_iota(jnp.int32, (slots, slots), 1)
@@ -216,41 +211,57 @@
         jnp.where(same, occ[...].astype(F32), 0.0), axis=1, keepdims=True
     )
 
-    lanes = lax.broadcasted_iota(jnp.int32, (heads, width), 1)
+    span = chunk * heads
+    lane_slot = lax.broadcasted_iota(jnp.int32, (chunk, span), 1) // heads
+    row_slot = lax.broadcasted_iota(jnp.int32, (chunk, span), 0)
+    own = (lane_slot == row_slot).astype(F32)
+    positions = lax.broadcasted_iota(jnp.int32, (width, span), 0).astype(F32)
+    slot_of_row = lax.broadcasted_iota(jnp.int32, (chunks, slots), 1)
+    chunk_of_row = lax.broadcasted_iota(jnp.int32, (chunks, slots), 0)
+    in_chunk = (slot_of_row // chunk == chunk_of_row).astype(F32)
+    spread = (
+        lax.broadcasted_iota(jnp.int32, (slots, span), 0) % chunk
+        == lax.broadcasted_iota(jnp.int32, (slots, span), 1) // heads
+    ).astype(F32)
+    lens_wide[...] = nn_dot(
+        (in_chunk * lens[...].astype(F32)).astype(BF), spread.astype(BF)
+    )
 
     def attend(c, carry):
-        k_copy(c).wait()
-        v_copy(c).wait()
-        scores, fresh, new_values = [], [], []
-        for p in range(CHUNK // 2):
-            slot = c * CHUNK + 2 * p
-            queries = qbuf[pl.ds(pl.multiple_of(slot * heads, 16), 2 * heads), :]
-            keys = kbuf[pl.ds(slot, 2)].reshape(2 * 128, width)
-            both = nt_dot(queries, keys) * inverse
-            wide = queries.astype(F32)
-            for b in range(2):
-                tile = both[b * heads : (b + 1) * heads, b * 128 : (b + 1) * 128]
-                scores.append(jnp.where(lanes < lens[0, slot + b], tile, -jnp.inf))
-                new_key = knf[pl.ds(slot + b, 1), :]
-                fresh.append(
-                    jnp.sum(
-                        wide[b * heads : (b + 1) * heads] * new_key,
-                        axis=1,
-                        keepdims=True,
-                    )
-                )
-        scores = jnp.concatenate(scores, axis=0)
-        fresh = jnp.concatenate(fresh, axis=0) * inverse
-        top = jnp.maximum(jnp.max(scores, axis=1, keepdims=True), fresh)
+        rows = pl.ds(pl.multiple_of(c * span, span), span)
+        first = c * chunk
+        for f in range(chunk // fetch):
+            k_copy(c * (chunk // fetch) + f).wait()
+        tiles = []
+        for p in range(chunk // 2):
+            pair_rows = pl.ds(pl.multiple_of((first + 2 * p) * heads, 16), 2 * heads)
+            keys = kbuf[pl.ds(first + 2 * p, 2)].reshape(2 * width, width)
+            both = nt_dot(qbuf[pair_rows, :], keys)
+            tiles += [both[:heads, :width], both[heads:, width:]]
+        products = jnp.concatenate(tiles, axis=0).T * inverse
+        new_keys = knb[pl.ds(pl.multiple_of(first, chunk), chunk), :]
+        fresh = jnp.sum(
+            own * nt_dot(new_keys, qbuf[rows, :]), axis=0, keepdims=True
+        ) * inverse
+        scores = jnp.where(
+            positions < lens_wide[pl.ds(c, 1), :], products, -jnp.inf
+        )
+        top = jnp.maximum(jnp.max(scores, axis=0, keepdims=True), fresh)
         scores_exp = jnp.exp(scores - top)
         fresh_exp = jnp.exp(fresh - top)
-        total = jnp.sum(scores_exp, axis=1, keepdims=True) + fresh_exp
+        total = jnp.sum(scores_exp, axis=0, keepdims=True) + fresh_exp
         scale = 1.0 / total
-        weights = scores_exp * scale
-        fresh_w = (fresh_exp * scale).astype(BF).astype(F32)
-        blank = jnp.zeros((heads, 128), F32)
-        for p in range(CHUNK // 2):
-            slot = c * CHUNK + 2 * p
+        weights = (scores_exp * scale).T
+        fresh_w = (own * (fresh_exp * scale)).astype(BF)
+        new_values = vnb[pl.ds(pl.multiple_of(first, chunk), chunk), :]
+        fresh_sum = lax.dot_general(
+            fresh_w, new_values, (((0,), (0,)), ((), ())), preferred_element_type=F32
+        )
+        blank = jnp.zeros((heads, width), F32)
+        for f in range(chunk // fetch):
+            v_copy(c * (chunk // fetch) + f).wait()
+        sums = []
+        for p in range(chunk // 2):
             r = 2 * p * heads
             pair = jnp.concatenate(
                 [
@@ -259,80 +270,62 @@
                 ],
                 axis=0,
             ).astype(BF)
-            values = vbuf[pl.ds(slot, 2)].reshape(2 * 128, width)
-            summed = nn_dot(pair, values)
-            for b in range(2):
-                new_value = vnf[pl.ds(slot + b, 1), :]
-                q = r + b * heads
-                obuf[pl.ds(pl.multiple_of((slot + b) * heads, heads), heads), :] = (
-                    summed[b * heads : (b + 1) * heads]
-                    + fresh_w[q : q + heads] * new_value
-                )
+            values = vbuf[pl.ds(first + 2 * p, 2)].reshape(2 * width, width)
+            sums.append(nn_dot(pair, values))
+        obuf[rows, :] = jnp.concatenate(sums, axis=0) + fresh_sum
         return carry
 
-    first = chunks // 2
-    lax.fori_loop(0, first, attend, 0)
-
-    pl.semaphore_wait(barrier, n - 1 + mp - 1)
-
-    def to_owner(out, landing, sems):
-        def copy(i):
-            peer = lax.rem(d + i, n)
+    attend(0, 0)
+    for i in range(mp):
+        w_copy(i).start()
+    lax.fori_loop(1, chunks, attend, 0)
+
+    class Exchange:
+        def __init__(self, out, landing, sems, over_dp, same_for_all=False):
+            self.count = n if over_dp else mp
+            self.out, self.landing, self.sems = out, landing, sems
+            self.over_dp, self.same_for_all = over_dp, same_for_all
+
+        def device(self, i):
+            return ((d + i) % n, m) if self.over_dp else (d, (m + i) % mp)
+
+        def start(self):
+            here = d if self.over_dp else m
+            for i in range(1, self.count):
+                device = self.device(i)
+                peer = device[0] if self.over_dp else device[1]
+                pltpu.make_async_remote_copy(
+                    src_ref=self.out if self.same_for_all else self.out.at[peer],
+                    dst_ref=self.landing.at[here],
+                    send_sem=self.sems.at[0],
+                    recv_sem=self.sems.at[1],
+                    device_id=device,
+                    device_id_type=MESH,
+                ).start()
+
+        def whole(self):
+            all_blocks = self.landing.at[pl.ds(0, self.count - 1)]
             return pltpu.make_async_remote_copy(
-                src_ref=out.at[peer],
-                dst_ref=landing.at[d],
-                send_sem=sems.at[0, i],
-                recv_sem=sems.at[1, i],
-                device_id=(peer, m),
+                src_ref=all_blocks,
+                dst_ref=all_blocks,
+                send_sem=self.sems.at[0],
+                recv_sem=self.sems.at[1],
+                device_id=self.device(1),
                 device_id_type=MESH,
             )
 
-        return copy
-
-    def over_mp(out, landing, sems, same_for_all):
-        def copy(i):
-            peer = lax.rem(m + i, mp)
-            return pltpu.make_async_remote_copy(
-                src_ref=out if same_for_all else out.at[peer],
-                dst_ref=landing.at[m],
-                send_sem=sems.at[0, i],
-                recv_sem=sems.at[1, i],
-                device_id=(d, peer),
-                device_id_type=MESH,
-            )
-
-        return copy
-
-    def start_all(copy, count):
-        def go(i, carry):
-            copy(i).start()
-            return carry
-
-        lax.fori_loop(1, count, go, 0)
-
-    def recv_all(copy, count):
-        def go(i, carry):
-            copy(i).wait_recv()
-            return carry
-
-        lax.fori_loop(1, count, go, 0)
-
-    def sent_all(copy, count):
-        def go(i, carry):
-            copy(i).wait_send()
-            return carry
-
-        lax.fori_loop(1, count, go, 0)
-
-    ids_copy = to_owner(ids_out, ids_in, ids_sems)
-    rows_copy = to_owner(rows_out, rows_in, rows_sems)
-    back_copy = to_owner(back_out, back_in, back_sems)
-    rs_copy = over_mp(rs_out, rs_in, rs_sems, False)
-    ag_copy = over_mp(ag_out, ag_in, ag_sems, True)
-
-    start_all(ids_copy, n)
-    lax.fori_loop(first, chunks, attend, 0)
-    ids_in[d] = ids_out[d]
+        def arrived(self):
+            self.whole().wait_recv()
+
+        def left(self):
+            self.whole().wait_send()
+
+    rows_ex = Exchange(rows_out, rows_in, rows_sems, True)
+    back_ex = Exchange(back_out, back_in, back_sems, True)
+    rs_ex = Exchange(rs_out, rs_in, rs_sems, False)
+    ag_ex = Exchange(ag_out, ag_in, ag_sems, False, True)
+
+    pl.semaphore_wait(barrier, n - 1 + mp - 1)
 
     for j in range(heads):
         cols = pl.ds(j * width, width)
@@ -340,7 +333,8 @@
         att[:, cols] = head
         sent = nn_dot(disp[...], head)
         rows_out[:, :, cols] = sent.reshape(n, cap, width).astype(BF)
-    start_all(rows_copy, n)
+    rows_ex.start()
+    rows_in[d] = rows_out[d]
 
     def block_product(i):
         w_copy(i).wait()
@@ -357,11 +351,11 @@
         return pl.ds(upper * side, side)
 
     def msg_copy(direction, i):
-        peer = lax.rem(m + (1 if direction == 0 else mp - 1), mp)
+        peer = (m + (1 if direction == 0 else mp - 1)) % mp
         return pltpu.make_async_remote_copy(
             src_ref=msg_out.at[direction, i],
             dst_ref=msg_in.at[direction, i],
-            send_sem=msg_send.at[direction, i],
+            send_sem=msg_send.at[0],
             recv_sem=msg_recv.at[direction, i],
             device_id=(d, peer),
             device_id_type=MESH,
@@ -390,12 +384,10 @@
                 base[rows, :] += msg_in[direction, last].astype(F32)
 
     def share_rows():
-        recv_all(ids_copy, n)
-        rows_in[d] = rows_out[d]
-        recv_all(rows_copy, n)
-        got = rows_in[...].astype(F32).reshape(codes, rows_in.shape[2]).astype(BF)
+        rows_ex.arrived()
+        got = rows_in[:, :, :features].astype(F32).reshape(codes, features).astype(BF)
         partial_low = nt_dot(got, shr[...])
-        which = ids_in[...].astype(F32).reshape(codes, 128)
+        which = rows_in[:, :, features:].astype(F32).reshape(codes, 128)
         row = lax.broadcasted_iota(jnp.int32, (codes, 128), 0)
         second = ((row // half_group) % 2).astype(F32)
         placed = jnp.where(which == second, partial_low, pltpu.roll(partial_low, 64, 1))
@@ -407,22 +399,22 @@
                 placed[r : r + half_group],
                 placed[r + half_group : r + group],
             )
-        start_all(rs_copy, mp)
+        rs_ex.start()
         rs_in[m] = rs_out[m]
 
     def sum_low():
-        recv_all(rs_copy, mp)
+        rs_ex.arrived()
         ag_out[...] = jnp.sum(rs_in[...], axis=0).astype(BF)
-        start_all(ag_copy, mp)
+        ag_ex.start()
         ag_in[m] = ag_out[...]
 
     def expand_low():
-        recv_all(ag_copy, mp)
+        ag_ex.arrived()
         low = ag_in[...].astype(F32)
         twice = jnp.concatenate(
             [low[g] for g in range(mp) for _ in range(2)], axis=0
         )
-        which = ids_in[...].astype(F32).reshape(codes, 128)
+        which = rows_in[:, :, features:].astype(F32).reshape(codes, 128)
         row = lax.broadcasted_iota(jnp.int32, (codes, 128), 0)
         second = ((row // half_group) % 2).astype(F32)
         lane_half = (
@@ -432,10 +424,9 @@
         kept = jnp.where(which == lane_half, moved, 0.0).astype(BF)
         delta = 0.5 * nn_dot(kept, expw[...])
         back_out[...] = delta.reshape(n, cap, outw).astype(BF)
-        start_all(back_copy, n)
+        back_ex.start()
         back_in[d] = back_out[d]
 
-    count = len(messages)
     block_product(0)
     send_message(0)
     block_product(1)
@@ -457,22 +448,21 @@
     expand_low()
     finish_base()
 
-    recv_all(back_copy, n)
+    back_ex.arrived()
     returned = back_in[...].astype(F32).reshape(codes, outw).astype(BF)
     correction = nn_dot(comb[...], returned)
     out_ref[...] = (live * (base[...] + correction)).astype(BF)
 
-    for copy, total_count in (
-        (ids_copy, n),
-        (rows_copy, n),
-        (back_copy, n),
-        (rs_copy, mp),
-        (ag_copy, mp),
-    ):
-        sent_all(copy, total_count)
-    for i in range(count):
-        for direction in range(2):
-            msg_copy(direction, i).wait_send()
+    for exchange in (rows_ex, back_ex, rs_ex, ag_ex):
+        exchange.left()
+    pltpu.make_async_remote_copy(
+        src_ref=msg_out,
+        dst_ref=msg_in,
+        send_sem=msg_send.at[0],
+        recv_sem=msg_recv.at[0, 0],
+        device_id=(d, (m + 1) % mp),
+        device_id_type=MESH,
+    ).wait_send()
 
 
 def solution(mesh):
@@ -501,18 +491,21 @@
         codes = n * cap
         ranks = shrink_weight.shape[0] * shrink_weight.shape[2]
         requests = request_adapter.shape[0]
-        chunks = slots // CHUNK
+        chunk = slots // 2
+        chunks = slots // chunk
+        fetch = slots // 8
+        fetches = slots // fetch
         messages = 2 * (mp // 2) - 1
         packed = codes // mp // 2
-        any_spec = pl.BlockSpec(memory_space=pl.ANY)
+        any_spec = pl.BlockSpec(memory_space=pltpu.HBM)
         dma = pltpu.SemaphoreType.DMA
         return pl.pallas_call(
             functools.partial(kernel, n, mp, cap),
-            out_shape=jax.ShapeDtypeStruct((slots, outw), BF),
+            out_shape=pltpu.VMEM((slots, outw), BF),
             in_specs=[any_spec] * 12,
             out_specs=pl.BlockSpec(memory_space=pltpu.VMEM),
             scratch_shapes=[
-                pltpu.SMEM((1, slots), jnp.int32),
+                pltpu.VMEM((1, slots), jnp.int32),
                 pltpu.VMEM((1, slots), jnp.int32),
                 pltpu.VMEM((1, slots), jnp.int32),
                 pltpu.VMEM((requests // 128, 128), jnp.int32),
@@ -521,8 +514,7 @@
                 pltpu.VMEM((slots, cached, width), BF),
                 pltpu.VMEM((slots, width), BF),
                 pltpu.VMEM((slots, width), BF),
-                pltpu.VMEM((slots, width), F32),
-                pltpu.VMEM((slots, width), F32),
+                pltpu.VMEM((chunks, chunk * heads), F32),
                 pltpu.VMEM((mp, features, outw), BF),
                 pltpu.VMEM((ranks, features), BF),
                 pltpu.VMEM((ranks, outw), BF),
@@ -530,10 +522,8 @@
                 pltpu.VMEM((slots, features), BF),
                 pltpu.VMEM((codes, slots), BF),
                 pltpu.VMEM((slots, codes), BF),
-                pltpu.VMEM((n, cap, 128), BF),
-                pltpu.VMEM((n, cap, 128), BF),
-                pltpu.VMEM((n, cap, features), BF),
-                pltpu.VMEM((n, cap, features), BF),
+                pltpu.VMEM((n, cap, features + 128), BF),
+                pltpu.VMEM((n, cap, features + 128), BF),
                 pltpu.VMEM((mp, slots, outw), F32),
                 pltpu.VMEM((2, messages, slots // 2, outw), BF),
                 pltpu.VMEM((2, messages, slots // 2, outw), BF),
@@ -545,21 +535,20 @@
                 pltpu.VMEM((n, cap, outw), BF),
                 pltpu.VMEM((n, cap, outw), BF),
                 dma((9,)),
-                dma((chunks,)),
-                dma((chunks,)),
+                dma((fetches,)),
+                dma((fetches,)),
                 dma((mp,)),
-                dma((2, n)),
-                dma((2, n)),
-                dma((2, mp)),
-                dma((2, mp)),
-                dma((2, n)),
-                dma((2, messages)),
+                dma((2,)),
+                dma((2,)),
+                dma((2,)),
+                dma((2,)),
+                dma((1,)),
                 dma((2, messages)),
             ],
             compiler_params=pltpu.CompilerParams(
                 collective_id=0,
                 has_side_effects=True,
-                vmem_limit_bytes=48 << 20,
+                vmem_limit_bytes=60 << 20,
             ),
         )(
             lengths.reshape(1, slots),

time: 54.6 us -> 41.3 us (0.76)
  local copies, waits for them, and re-layouts: 9.84 us -> 0.66 us
  Pallas kernels: 44.3 us -> 40.5 us
    unnamed x21 -> x1, local copies, waits for them, and re-layouts: 9.84 us -> 0.66 us
    pallas_call x1, Pallas kernels: 44.3 us -> 40.5 us  [body(): pl.pallas_call(functools.partial(kernel, n, mp, cap), out_shape=pltpu.VME...]
where the time goes in v2:
time: 41.3 us; the launch traced here: 41.2 us
  Pallas kernels  40.5 us (98%)
  local copies, waits for them, and re-layouts  0.66 us (2%)
    pallas_call x1, Pallas kernels, body(): pl.pallas_call(functools.partial(kernel, n, mp, cap), out_shape=pltpu.VME...  40.5 us

profile of v2, /device:TPU:1, one launch (start us, length us, event | category | flops | bytes accessed | tf_op | source)
XLA Modules:
  0.0 41.2 jit_solution(3846468480341095268)
XLA Ops:
  0.0 40.5 %shard_map.118 = bf16[128,512]{1,0:T(8,128)(2,1)S(1)} custom-call(s32[1,128]{1,0:T(1,128)} %bitcast.21, s32[1,128]{1,0:T(1,128)} %bitcast.22, s32[1,128]{1,0:T(1,128)} %bitcast.23, s32[32,128]{1,0:T(8,128)} %bitcast.20, bf16[1024,128]{1,0:T(8,128)(2,1)} %bitcast.15, bf16[128,128,128]{2,1,0:T(8,128)(2,1)} %bitcast.13, bf16[128,128,128]{2,1,0:T(8,128)(2,1)} %bitcast.14, ...), custom_call_target="tpu_custom_call" | custom-call | tf_op jit(solution)/shard_map/pallas_call | solution.py:502
  40.5 0.7 %copy.14 = bf16[128,512]{1,0:T(8,128)(2,1)} copy(bf16[128,512]{1,0:T(8,128)(2,1)S(1)} %shard_map.118) | data formatting | bytes 262144

commit v3 on v2

--- a/solution.py
+++ b/solution.py
@@ -97,7 +97,7 @@
     half_group = group // 2
     half = mp // 2
     inverse = 1.0 / math.sqrt(width)
-    chunk = slots // 2
+    chunk = slots
     chunks = slots // chunk
     fetch = slots // 8
     fetches = slots // fetch
@@ -140,12 +140,11 @@
 
     for copy in smalls[:4]:
         copy.start()
-    k_copy(0).start()
-    v_copy(0).start()
+    for c in range(fetches):
+        k_copy(c).start()
     for copy in smalls[4:]:
         copy.start()
-    for c in range(1, fetches):
-        k_copy(c).start()
+    for c in range(fetches):
         v_copy(c).start()
 
     barrier = pltpu.get_barrier_semaphore()
@@ -258,6 +257,8 @@
             fresh_w, new_values, (((0,), (0,)), ((), ())), preferred_element_type=F32
         )
         blank = jnp.zeros((heads, width), F32)
+        for i in range(mp):
+            w_copy(i).start()
         for f in range(chunk // fetch):
             v_copy(c * (chunk // fetch) + f).wait()
         sums = []
@@ -276,9 +277,21 @@
         return carry
 
     attend(0, 0)
-    for i in range(mp):
-        w_copy(i).start()
-    lax.fori_loop(1, chunks, attend, 0)
+
+    ring = math.isqrt(n // 2)
+
+    def peer_of(i):
+        dx, dy, dc = i // (2 * ring), (i // 2) % ring, i % 2
+        x = (d // (2 * ring) + dx) % ring
+        y = ((d // 2) % ring + dy) % ring
+        return (x * ring + y) * 2 + (d + dc) % 2
+
+    def hops(i):
+        dx, dy = i // (2 * ring), (i // 2) % ring
+        return min(dx, ring - dx) + min(dy, ring - dy)
+
+    far_first_dp = sorted(range(1, n), key=lambda i: -hops(i))
+    far_first_mp = sorted(range(1, mp), key=lambda i: -min(i, mp - i))
 
     class Exchange:
         def __init__(self, out, landing, sems, over_dp, same_for_all=False):
@@ -287,11 +300,13 @@
             self.over_dp, self.same_for_all = over_dp, same_for_all
 
         def device(self, i):
-            return ((d + i) % n, m) if self.over_dp else (d, (m + i) % mp)
+            if not self.over_dp:
+                return (d, (m + i) % mp)
+            return (peer_of(i), m)
 
         def start(self):
             here = d if self.over_dp else m
-            for i in range(1, self.count):
+            for i in far_first_dp if self.over_dp else far_first_mp:
                 device = self.device(i)
                 peer = device[0] if self.over_dp else device[1]
                 pltpu.make_async_remote_copy(
@@ -432,16 +447,14 @@
     block_product(1)
     block_product(2)
     send_message(1)
-    block_product(3)
-    block_product(4)
-    send_message(2)
-    block_product(5)
-    block_product(6)
-    send_message(3)
+    for i in range(3, mp - 1):
+        block_product(i)
     w_copy(mp - 1).wait()
     base[...] = nn_dot(att[...], wbuf[mp - 1])
+    send_message(2)
+    send_message(3)
+    share_rows()
     send_message(4)
-    share_rows()
     send_message(5)
     sum_low()
     send_message(6)
@@ -491,7 +504,7 @@
         codes = n * cap
         ranks = shrink_weight.shape[0] * shrink_weight.shape[2]
         requests = request_adapter.shape[0]
-        chunk = slots // 2
+        chunk = slots
         chunks = slots // chunk
         fetch = slots // 8
         fetches = slots // fetch

time: 41.3 us -> 38.6 us (0.935)
  Pallas kernels: 40.5 us -> 37.8 us
    pallas_call x1, Pallas kernels: 40.5 us -> 37.8 us  [body(): pl.pallas_call(functools.partial(kernel, n, mp, cap), out_shape=pltpu.VME...]
where the time goes in v3:
time: 38.6 us; the launch traced here: 38.5 us
  Pallas kernels  37.8 us (98%)
  local copies, waits for them, and re-layouts  0.66 us (2%)
    pallas_call x1, Pallas kernels, body(): pl.pallas_call(functools.partial(kernel, n, mp, cap), out_shape=pltpu.VME...  37.8 us

profile of v3, /device:TPU:1, one launch (start us, length us, event | category | flops | bytes accessed | tf_op | source)
XLA Modules:
  0.0 38.5 jit_solution(17920383100131415535)
XLA Ops:
  0.0 37.8 %shard_map.118 = bf16[128,512]{1,0:T(8,128)(2,1)S(1)} custom-call(s32[1,128]{1,0:T(1,128)} %bitcast.21, s32[1,128]{1,0:T(1,128)} %bitcast.22, s32[1,128]{1,0:T(1,128)} %bitcast.23, s32[32,128]{1,0:T(8,128)} %bitcast.20, bf16[1024,128]{1,0:T(8,128)(2,1)} %bitcast.15, bf16[128,128,128]{2,1,0:T(8,128)(2,1)} %bitcast.13, bf16[128,128,128]{2,1,0:T(8,128)(2,1)} %bitcast.14, ...), custom_call_target="tpu_custom_call" | custom-call | tf_op jit(solution)/shard_map/pallas_call | solution.py:515
  37.8 0.7 %copy.14 = bf16[128,512]{1,0:T(8,128)(2,1)} copy(bf16[128,512]{1,0:T(8,128)(2,1)S(1)} %shard_map.118) | data formatting | bytes 262144

commit v4 on v3

--- a/solution.py
+++ b/solution.py
@@ -80,7 +80,8 @@
     w_sem,
     rows_sems,
     rs_sems,
-    ag_sems,
+    ag_send,
+    ag_recv,
     back_sems,
     msg_send,
     msg_recv,
@@ -338,7 +339,17 @@
     rows_ex = Exchange(rows_out, rows_in, rows_sems, True)
     back_ex = Exchange(back_out, back_in, back_sems, True)
     rs_ex = Exchange(rs_out, rs_in, rs_sems, False)
-    ag_ex = Exchange(ag_out, ag_in, ag_sems, False, True)
+
+    def low_copy(i):
+        return pltpu.make_async_remote_copy(
+            src_ref=ag_out,
+            dst_ref=ag_in.at[i],
+            send_sem=ag_send.at[0],
+            recv_sem=ag_recv.at[i],
+            device_id=(d, (m + i) % mp),
+            device_id_type=MESH,
+        )
+
 
     pl.semaphore_wait(barrier, n - 1 + mp - 1)
 
@@ -420,26 +431,49 @@
     def sum_low():
         rs_ex.arrived()
         ag_out[...] = jnp.sum(rs_in[...], axis=0).astype(BF)
-        ag_ex.start()
-        ag_in[m] = ag_out[...]
-
-    def expand_low():
-        ag_ex.arrived()
-        low = ag_in[...].astype(F32)
-        twice = jnp.concatenate(
-            [low[g] for g in range(mp) for _ in range(2)], axis=0
-        )
-        which = rows_in[:, :, features:].astype(F32).reshape(codes, 128)
-        row = lax.broadcasted_iota(jnp.int32, (codes, 128), 0)
-        second = ((row // half_group) % 2).astype(F32)
-        lane_half = (
-            lax.broadcasted_iota(jnp.int32, (codes, 128), 1) // 64
-        ).astype(F32)
-        moved = jnp.where(which == second, twice, pltpu.roll(twice, 64, 1))
+        for i in far_first_mp:
+            low_copy(i).start()
+        ag_in[0] = ag_out[...]
+
+    sources = group // cap
+    row = lax.broadcasted_iota(jnp.int32, (group, 128), 0)
+    second_half = (row // half_group).astype(F32)
+    lane_half = (lax.broadcasted_iota(jnp.int32, (group, 128), 1) // 64).astype(F32)
+
+    def expand_group(i):
+        if i:
+            low_copy(i).wait_recv()
+        first_source = ((m + mp - i) % mp) * sources
+        low = ag_in[i].astype(F32)
+        twice = jnp.concatenate([low, low], axis=0)
+        which = (
+            rows_in[pl.ds(first_source, sources), :, features:]
+            .astype(F32)
+            .reshape(group, 128)
+        )
+        moved = jnp.where(which == second_half, twice, pltpu.roll(twice, 64, 1))
         kept = jnp.where(which == lane_half, moved, 0.0).astype(BF)
         delta = 0.5 * nn_dot(kept, expw[...])
-        back_out[...] = delta.reshape(n, cap, outw).astype(BF)
-        back_ex.start()
+        back_out[pl.ds(first_source, sources)] = delta.reshape(
+            sources, cap, outw
+        ).astype(BF)
+        for k in range(sources):
+            source = first_source + k
+
+            @pl.when(source != d)
+            def _():
+                pltpu.make_async_remote_copy(
+                    src_ref=back_out.at[source],
+                    dst_ref=back_in.at[d],
+                    send_sem=back_sems.at[0],
+                    recv_sem=back_sems.at[1],
+                    device_id=(source, m),
+                    device_id_type=MESH,
+                ).start()
+
+    def expand_low():
+        for i in sorted(range(mp), key=lambda i: min(i, mp - i)):
+            expand_group(i)
         back_in[d] = back_out[d]
 
     block_product(0)
@@ -466,8 +500,17 @@
     correction = nn_dot(comb[...], returned)
     out_ref[...] = (live * (base[...] + correction)).astype(BF)
 
-    for exchange in (rows_ex, back_ex, rs_ex, ag_ex):
+    for exchange in (rows_ex, back_ex, rs_ex):
         exchange.left()
+    low_sent = ag_in.at[pl.ds(0, mp - 1)]
+    pltpu.make_async_remote_copy(
+        src_ref=low_sent,
+        dst_ref=low_sent,
+        send_sem=ag_send.at[0],
+        recv_sem=ag_recv.at[1],
+        device_id=(d, (m + 1) % mp),
+        device_id_type=MESH,
+    ).wait_send()
     pltpu.make_async_remote_copy(
         src_ref=msg_out,
         dst_ref=msg_in,
@@ -553,7 +596,8 @@
                 dma((mp,)),
                 dma((2,)),
                 dma((2,)),
-                dma((2,)),
+                dma((1,)),
+                dma((mp,)),
                 dma((2,)),
                 dma((1,)),
                 dma((2, messages)),

time: 38.6 us -> 37.2 us (0.964)
  the two profiles are of different devices: /device:TPU:1 before, /device:TPU:5 now
where the time goes in v4:
time: 37.2 us
  Pallas kernels  36.5 us (98%)
  local copies, waits for them, and re-layouts  0.66 us (2%)
    pallas_call x1, Pallas kernels, body(): pl.pallas_call(functools.partial(kernel, n, mp, cap), out_shape=pltpu.VME...  36.5 us

profile of v4, /device:TPU:5, one launch (start us, length us, event | category | flops | bytes accessed | tf_op | source)
XLA Modules:
  0.0 37.2 jit_solution(13336296913063856560)
XLA Ops:
  0.0 36.5 %shard_map.118 = bf16[128,512]{1,0:T(8,128)(2,1)S(1)} custom-call(s32[1,128]{1,0:T(1,128)} %bitcast.21, s32[1,128]{1,0:T(1,128)} %bitcast.22, s32[1,128]{1,0:T(1,128)} %bitcast.23, s32[32,128]{1,0:T(8,128)} %bitcast.20, bf16[1024,128]{1,0:T(8,128)(2,1)} %bitcast.15, bf16[128,128,128]{2,1,0:T(8,128)(2,1)} %bitcast.13, bf16[128,128,128]{2,1,0:T(8,128)(2,1)} %bitcast.14, ...), custom_call_target="tpu_custom_call" | custom-call | tf_op jit(solution)/shard_map/pallas_call | solution.py:558
  36.5 0.7 %copy.14 = bf16[128,512]{1,0:T(8,128)(2,1)} copy(bf16[128,512]{1,0:T(8,128)(2,1)S(1)} %shard_map.118) | data formatting | bytes 262144

commit v5 on v4

--- a/solution.py
+++ b/solution.py
@@ -424,13 +424,13 @@
                 lane < 64,
                 placed[r : r + half_group],
                 placed[r + half_group : r + group],
-            )
+            ).astype(BF)
         rs_ex.start()
         rs_in[m] = rs_out[m]
 
     def sum_low():
         rs_ex.arrived()
-        ag_out[...] = jnp.sum(rs_in[...], axis=0).astype(BF)
+        ag_out[...] = jnp.sum(rs_in[...].astype(F32), axis=0).astype(BF)
         for i in far_first_mp:
             low_copy(i).start()
         ag_in[0] = ag_out[...]
@@ -584,8 +584,8 @@
                 pltpu.VMEM((2, messages, slots // 2, outw), BF),
                 pltpu.VMEM((2, messages, slots // 2, outw), BF),
                 pltpu.VMEM((slots, outw), F32),
-                pltpu.VMEM((mp, packed, 128), F32),
-                pltpu.VMEM((mp, packed, 128), F32),
+                pltpu.VMEM((mp, packed, 128), BF),
+                pltpu.VMEM((mp, packed, 128), BF),
                 pltpu.VMEM((packed, 128), BF),
                 pltpu.VMEM((mp, packed, 128), BF),
                 pltpu.VMEM((n, cap, outw), BF),

time: 37.2 us -> 36.5 us (0.981)
  Pallas kernels: 36.5 us -> 35.8 us
    pallas_call x1, Pallas kernels: 36.5 us -> 35.8 us  [body(): pl.pallas_call(functools.partial(kernel, n, mp, cap), out_shape=pltpu.VME...]
where the time goes in v5:
time: 36.5 us
  Pallas kernels  35.8 us (98%)
  local copies, waits for them, and re-layouts  0.66 us (2%)
    pallas_call x1, Pallas kernels, body(): pl.pallas_call(functools.partial(kernel, n, mp, cap), out_shape=pltpu.VME...  35.8 us

profile of v5, /device:TPU:5, one launch (start us, length us, event | category | flops | bytes accessed | tf_op | source)
XLA Modules:
  0.0 36.5 jit_solution(13700324934271123016)
XLA Ops:
  0.0 35.8 %shard_map.118 = bf16[128,512]{1,0:T(8,128)(2,1)S(1)} custom-call(s32[1,128]{1,0:T(1,128)} %bitcast.21, s32[1,128]{1,0:T(1,128)} %bitcast.22, s32[1,128]{1,0:T(1,128)} %bitcast.23, s32[32,128]{1,0:T(8,128)} %bitcast.20, bf16[1024,128]{1,0:T(8,128)(2,1)} %bitcast.15, bf16[128,128,128]{2,1,0:T(8,128)(2,1)} %bitcast.13, bf16[128,128,128]{2,1,0:T(8,128)(2,1)} %bitcast.14, ...), custom_call_target="tpu_custom_call" | custom-call | tf_op jit(solution)/shard_map/pallas_call | solution.py:558
  35.8 0.7 %copy.14 = bf16[128,512]{1,0:T(8,128)(2,1)} copy(bf16[128,512]{1,0:T(8,128)(2,1)S(1)} %shard_map.118) | data formatting | bytes 262144
